TPU v7x, 32 devices: a whole 2x2x4 slice. The times are simulated.
32 devices in a mesh: dp: 8 (over z, x), mp: 4 (over y, core).
Axes of the slice: x: 2, y: 2, z: 4, core: 2. Of those that a mesh axis runs over, the one named last changes fastest.
Arguments:
- text_blocks: bfloat16 [256, 64, 768], P(('dp', 'mp')), may hold values from -6 to 6
- visual_blocks: bfloat16 [256, 40, 768], P(('dp', 'mp')), may hold values from -6 to 6
- drop_flags: int32 [256, 2], P('dp'), may hold values 0 or 1
- qkv_weight: bfloat16 [4, 768, 3, 768], P(None, None, None, 'mp'), may hold values from -0.21875 to 0.21875
- out_weight: bfloat16 [4, 768, 768], P(None, 'mp'), may hold values from -0.625 to 0.625
- up_weight: bfloat16 [2, 768, 3072], P(None, None, 'mp'), may hold values from -0.21875 to 0.21875
- down_weight: bfloat16 [2, 3072, 768], P(None, 'mp'), may hold values from -0.109375 to 0.109375
- norm_gain: float32 [6, 768], replicated, may hold values from 0.5 to 1.5
- norm_shift: float32 [6, 768], replicated, may hold values from -3 to 3
- text_cotangent: bfloat16 [256, 64, 768], P(('dp', 'mp')), may hold values from -6 to 6
- visual_cotangent: bfloat16 [256, 40, 768], P(('dp', 'mp')), may hold values from -6 to 6
Outputs:
- text_output: bfloat16 [256, 64, 768], P(('dp', 'mp'))
- visual_output: bfloat16 [256, 40, 768], P(('dp', 'mp'))
- text_gradient: bfloat16 [256, 64, 768], P(('dp', 'mp'))
- visual_gradient: bfloat16 [256, 40, 768], P(('dp', 'mp'))
- qkv_gradient: float32 [4, 768, 3, 768], P(None, None, None, 'mp')
- out_gradient: float32 [4, 768, 768], P(None, 'mp')
- up_gradient: float32 [2, 768, 3072], P(None, None, 'mp')
- down_gradient: float32 [2, 3072, 768], P(None, 'mp')
- gain_gradient: float32 [6, 768], replicated
- shift_gradient: float32 [6, 768], replicated
Inputs may be any that keep to these rules, and one draw needn't show every extreme that they name: drop_flags[:, 0] = 1 marks a page whose text is absent, drop_flags[:, 1] = 1 one whose visual blocks are absent.
All inputs are finite; a program needn't handle non-finite values.
Results may differ from a plain program's by a relative error of at most 0.025.
Values may be sent and summed in bfloat16 or wider, within the bound.
No kernel may reach another device: no remote copies, remote signals or barrier semaphores. Data moves between devices by JAX's collectives and lax.ppermute only.
A program may use at most 256 MiB of HBM per device.

v0:
```python
import jax
import jax.numpy as jnp
from jax import lax
from jax.sharding import PartitionSpec as P

HEAD = 64
EPSILON = 1e-05


def normalize(values, gain, shift):
    center = values - jnp.mean(values, axis=-1, keepdims=True)
    spread = jnp.mean(center * center, axis=-1, keepdims=True)
    return center * lax.rsqrt(spread + EPSILON) * gain + shift


def linear(activation, weight):
    return jnp.einsum("pld,de->ple", activation, weight, preferred_element_type=jnp.float32)


def linear_back(gradient, weight):
    return jnp.einsum("ple,de->pld", gradient, weight, preferred_element_type=jnp.float32)


def weight_grad(activation, gradient):
    return jnp.einsum("pld,ple->de", activation, gradient, preferred_element_type=jnp.float32)


def split_heads(values):
    return values.reshape(values.shape[0], values.shape[1], values.shape[2] // HEAD, HEAD)


def merge_heads(values):
    return values.reshape(values.shape[0], values.shape[1], values.shape[2] * values.shape[3])


def score_block(queries, key_block):
    raw = jnp.einsum(
        "pqhe,pkhe->phqk",
        split_heads(queries),
        split_heads(key_block),
        preferred_element_type=jnp.float32,
    )
    return raw * HEAD ** (-0.5)


def attend_context(query_side, key_side, weight_block, keep_mask):
    queries = linear(query_side, weight_block[:, 0]).astype(jnp.bfloat16)
    key_block = linear(key_side, weight_block[:, 1]).astype(jnp.bfloat16)
    value_block = linear(key_side, weight_block[:, 2]).astype(jnp.bfloat16)
    scores = score_block(queries, key_block)
    row_max = jnp.max(scores, axis=-1, keepdims=True)
    log_total = row_max + jnp.log(jnp.sum(jnp.exp(scores - row_max), axis=-1, keepdims=True))
    probability = jnp.exp(scores - log_total).astype(jnp.bfloat16)
    context = merge_heads(
        jnp.einsum(
            "phqk,pkhe->pqhe",
            probability,
            split_heads(value_block),
            preferred_element_type=jnp.float32,
        )
    )
    if keep_mask is not None:
        context = context * keep_mask[:, None, None]
    context = context.astype(jnp.bfloat16)
    return (context, (queries, key_block, value_block, log_total, context))


def attend_back(query_side, key_side, weight_block, out_block, keep_mask, saved, out_grad):
    queries, key_block, value_block, log_total, context = saved
    out_weight_grad = weight_grad(context, out_grad)
    context_grad = linear_back(out_grad, out_block).astype(jnp.bfloat16)
    if keep_mask is not None:
        context_grad = context_grad * keep_mask[:, None, None].astype(jnp.bfloat16)
    probability = jnp.exp(score_block(queries, key_block) - log_total)
    heads_grad = split_heads(context_grad)
    prob_grad = jnp.einsum(
        "pqhe,pkhe->phqk", heads_grad, split_heads(value_block), preferred_element_type=jnp.float32
    )
    value_grad = merge_heads(
        jnp.einsum(
            "phqk,pqhe->pkhe",
            probability.astype(jnp.bfloat16),
            heads_grad,
            preferred_element_type=jnp.float32,
        )
    ).astype(jnp.bfloat16)
    score_grad = (
        probability * (prob_grad - jnp.sum(prob_grad * probability, axis=-1, keepdims=True))
    ).astype(jnp.bfloat16)
    query_grad = (
        merge_heads(
            jnp.einsum(
                "phqk,pkhe->pqhe",
                score_grad,
                split_heads(key_block),
                preferred_element_type=jnp.float32,
            )
        )
        * HEAD ** (-0.5)
    ).astype(jnp.bfloat16)
    key_grad = (
        merge_heads(
            jnp.einsum(
                "phqk,pqhe->pkhe",
                score_grad,
                split_heads(queries),
                preferred_element_type=jnp.float32,
            )
        )
        * HEAD ** (-0.5)
    ).astype(jnp.bfloat16)
    in_weight_grad = jnp.stack(
        [
            weight_grad(query_side, query_grad),
            weight_grad(key_side, key_grad),
            weight_grad(key_side, value_grad),
        ],
        axis=1,
    )
    query_back = linear_back(query_grad, weight_block[:, 0])
    key_back = linear_back(key_grad, weight_block[:, 1]) + linear_back(
        value_grad, weight_block[:, 2]
    )
    return (in_weight_grad, out_weight_grad, query_back, key_back)


def feed_forward(activation, up_block, down_block):
    before = linear(activation, up_block)
    hidden = jax.nn.gelu(before).astype(jnp.bfloat16)
    return (linear(hidden, down_block), (before, hidden))


def feed_back(activation, up_block, down_block, saved, out_grad):
    before, hidden = saved
    down_grad = weight_grad(hidden, out_grad)
    hidden_grad = linear_back(out_grad, down_block)
    gelu_pull = jax.vjp(jax.nn.gelu, before)[1]
    before_grad = gelu_pull(hidden_grad)[0].astype(jnp.bfloat16)
    up_grad = weight_grad(activation, before_grad)
    return (up_grad, down_grad, linear_back(before_grad, up_block))


def per_device(
    text_blocks,
    visual_blocks,
    drop_flags,
    qkv_weight,
    out_weight,
    up_weight,
    down_weight,
    norm_gain,
    norm_shift,
    text_cotangent,
    visual_cotangent,
):
    keep_text = (1 - drop_flags[:, 0]).astype(jnp.float32)
    keep_visual = (1 - drop_flags[:, 1]).astype(jnp.float32)
    text_now = text_blocks.astype(jnp.float32)
    visual_now = visual_blocks.astype(jnp.float32)
    inputs = []
    gathered = []
    saved = []
    for sublayer in range(3):
        inputs.append((text_now, visual_now))
        text_norm = normalize(text_now, norm_gain[2 * sublayer], norm_shift[2 * sublayer]).astype(
            jnp.bfloat16
        )
        visual_norm = normalize(
            visual_now, norm_gain[2 * sublayer + 1], norm_shift[2 * sublayer + 1]
        ).astype(jnp.bfloat16)
        text_rows, visual_rows = (
            lax.all_gather(text_norm, "mp", axis=0, tiled=True),
            lax.all_gather(visual_norm, "mp", axis=0, tiled=True),
        )
        gathered.append((text_rows, visual_rows))
        text_part = None
        visual_part = None
        if sublayer < 2:
            if sublayer == 0:
                text_context, text_saved = attend_context(
                    text_rows, visual_rows, qkv_weight[0], keep_visual
                )
                visual_context, visual_saved = attend_context(
                    visual_rows, text_rows, qkv_weight[1], keep_text
                )
            else:
                text_context, text_saved = attend_context(text_rows, text_rows, qkv_weight[2], None)
                visual_context, visual_saved = attend_context(
                    visual_rows, visual_rows, qkv_weight[3], None
                )
            text_part = linear(text_context, out_weight[2 * sublayer])
            visual_part = linear(visual_context, out_weight[2 * sublayer + 1])
        else:
            text_part, text_saved = feed_forward(text_rows, up_weight[0], down_weight[0])
            visual_part, visual_saved = feed_forward(visual_rows, up_weight[1], down_weight[1])
        text_added, visual_added = (
            lax.psum_scatter(
                text_part.astype(jnp.bfloat16), "mp", scatter_dimension=0, tiled=True
            ).astype(jnp.float32),
            lax.psum_scatter(
                visual_part.astype(jnp.bfloat16), "mp", scatter_dimension=0, tiled=True
            ).astype(jnp.float32),
        )
        saved.append((text_saved, visual_saved))
        text_now = text_now + text_added
        visual_now = visual_now + visual_added
    text_output = text_now.astype(jnp.bfloat16)
    visual_output = visual_now.astype(jnp.bfloat16)
    text_back = text_cotangent.astype(jnp.float32)
    visual_back = visual_cotangent.astype(jnp.float32)
    in_parts = [None, None, None, None]
    out_parts = [None, None, None, None]
    gain_parts = [None, None, None, None, None, None]
    shift_parts = [None, None, None, None, None, None]
    up_grads = None
    down_grads = None
    for sublayer in (2, 1, 0):
        text_branch, visual_branch = (
            lax.all_gather(text_back.astype(jnp.bfloat16), "mp", axis=0, tiled=True),
            lax.all_gather(visual_back.astype(jnp.bfloat16), "mp", axis=0, tiled=True),
        )
        text_rows, visual_rows = gathered[sublayer]
        text_saved, visual_saved = saved[sublayer]
        if sublayer == 2:
            up_text, down_text, text_part = feed_back(
                text_rows, up_weight[0], down_weight[0], text_saved, text_branch
            )
            up_visual, down_visual, visual_part = feed_back(
                visual_rows, up_weight[1], down_weight[1], visual_saved, visual_branch
            )
            up_grads = jnp.stack([up_text, up_visual])
            down_grads = jnp.stack([down_text, down_visual])
        elif sublayer == 1:
            in_parts[2], out_parts[2], query_back, key_back = attend_back(
                text_rows, text_rows, qkv_weight[2], out_weight[2], None, text_saved, text_branch
            )
            text_part = query_back + key_back
            in_parts[3], out_parts[3], query_back, key_back = attend_back(
                visual_rows,
                visual_rows,
                qkv_weight[3],
                out_weight[3],
                None,
                visual_saved,
                visual_branch,
            )
            visual_part = query_back + key_back
        else:
            in_parts[0], out_parts[0], text_query_back, visual_key_back = attend_back(
                text_rows,
                visual_rows,
                qkv_weight[0],
                out_weight[0],
                keep_visual,
                text_saved,
                text_branch,
            )
            in_parts[1], out_parts[1], visual_query_back, text_key_back = attend_back(
                visual_rows,
                text_rows,
                qkv_weight[1],
                out_weight[1],
                keep_text,
                visual_saved,
                visual_branch,
            )
            text_part = text_query_back + text_key_back
            visual_part = visual_query_back + visual_key_back
        text_norm_grad, visual_norm_grad = (
            lax.psum_scatter(
                text_part.astype(jnp.bfloat16), "mp", scatter_dimension=0, tiled=True
            ).astype(jnp.float32),
            lax.psum_scatter(
                visual_part.astype(jnp.bfloat16), "mp", scatter_dimension=0, tiled=True
            ).astype(jnp.float32),
        )
        text_in, visual_in = inputs[sublayer]
        text_pull = jax.vjp(normalize, text_in, norm_gain[2 * sublayer], norm_shift[2 * sublayer])[
            1
        ]
        text_delta, gain_parts[2 * sublayer], shift_parts[2 * sublayer] = text_pull(text_norm_grad)
        visual_pull = jax.vjp(
            normalize, visual_in, norm_gain[2 * sublayer + 1], norm_shift[2 * sublayer + 1]
        )[1]
        visual_delta, gain_parts[2 * sublayer + 1], shift_parts[2 * sublayer + 1] = visual_pull(
            visual_norm_grad
        )
        text_back = text_back + text_delta
        visual_back = visual_back + visual_delta
    gain_grads = jnp.stack(gain_parts)
    shift_grads = jnp.stack(shift_parts)
    gain_grads, shift_grads = (
        lax.psum(gain_grads.astype(jnp.bfloat16), "mp").astype(jnp.float32),
        lax.psum(shift_grads.astype(jnp.bfloat16), "mp").astype(jnp.float32),
    )
    in_grads = jnp.stack(in_parts)
    out_grads = jnp.stack(out_parts)
    in_grads, out_grads, up_grads, down_grads = jax.tree.map(
        lambda grad: lax.psum(grad.astype(jnp.bfloat16), "dp").astype(jnp.float32),
        (in_grads, out_grads, up_grads, down_grads),
    )
    gain_grads, shift_grads = lax.psum((gain_grads, shift_grads), "dp")
    return (
        text_output,
        visual_output,
        text_back.astype(jnp.bfloat16),
        visual_back.astype(jnp.bfloat16),
        in_grads,
        out_grads,
        up_grads,
        down_grads,
        gain_grads,
        shift_grads,
    )


def solution(mesh):
    placed = (
        P(("dp", "mp"), None, None),
        P(("dp", "mp"), None, None),
        P("dp", None),
        P(None, None, None, "mp"),
        P(None, "mp", None),
        P(None, None, "mp"),
        P(None, "mp", None),
        P(),
        P(),
        P(("dp", "mp"), None, None),
        P(("dp", "mp"), None, None),
    )
    return jax.shard_map(
        per_device,
        mesh=mesh,
        in_specs=placed,
        out_specs=(
            P(("dp", "mp"), None, None),
            P(("dp", "mp"), None, None),
            P(("dp", "mp"), None, None),
            P(("dp", "mp"), None, None),
            P(None, None, None, "mp"),
            P(None, "mp", None),
            P(None, None, "mp"),
            P(None, "mp", None),
            P(),
            P(),
        ),
        check_vma=False,
    )
```

profile of v0, /device:TPU:0, one launch (start us, length us, event | category | flops | bytes accessed | tf_op | source)
XLA Modules:
  0.0 1164.1 jit_solution(13793235685979987641)
XLA Ops:
  20.7 18.6 %all-gather.13.cloned.1.call-done = bf16[32,40,768]{2,1,0:T(8,128)(2,1)} async-done(((bf16[8,40,768]{2,1,0:T(8,128)(2,1)}), bf16[32,40,768]{2,1,0:T(8,128)(2,1)}) %all-gather.13.cloned.1.call-update) | async-done | bytes 1966096 | tf_op jit(solution)/shard_map/all_gather | solution.py:173
  42.8 27.1 %all-gather.15.cloned.1.call-done = bf16[32,64,768]{2,1,0:T(8,128)(2,1)} async-done(((bf16[8,64,768]{2,1,0:T(8,128)(2,1)}), bf16[32,64,768]{2,1,0:T(8,128)(2,1)}) %all-gather.15.cloned.1.call-update) | async-done | bytes 3145744 | tf_op jit(solution)/shard_map/all_gather | solution.py:172
  127.7 37.1 %reduce-scatter.13.cloned.1.call-done = bf16[8,64,768]{2,1,0:T(8,128)(2,1)} async-done(((bf16[32,64,768]{2,1,0:T(8,128)(2,1)}), bf16[8,64,768]{2,1,0:T(8,128)(2,1)}) %reduce-scatter.13.cloned.1.call-update) | async-done | bytes 786448 | tf_op jit(solution)/shard_map/reduce_scatter | solution.py:197
  168.6 20.0 %all-gather.21.cloned.1.call-done = bf16[32,40,768]{2,1,0:T(8,128)(2,1)} async-done(((bf16[8,40,768]{2,1,0:T(8,128)(2,1)}), bf16[32,40,768]{2,1,0:T(8,128)(2,1)}) %all-gather.21.cloned.1.call-update) | async-done | bytes 1966096 | tf_op jit(solution)/shard_map/all_gather | solution.py:173
  256.6 37.1 %reduce-scatter.15.cloned.1.call-done = bf16[8,64,768]{2,1,0:T(8,128)(2,1)} async-done(((bf16[32,64,768]{2,1,0:T(8,128)(2,1)}), bf16[8,64,768]{2,1,0:T(8,128)(2,1)}) %reduce-scatter.15.cloned.1.call-update) | async-done | bytes 786448 | tf_op jit(solution)/shard_map/reduce_scatter | solution.py:197
  297.9 19.9 %all-gather.23.cloned.1.call-done = bf16[32,40,768]{2,1,0:T(8,128)(2,1)} async-done(((bf16[8,40,768]{2,1,0:T(8,128)(2,1)}), bf16[32,40,768]{2,1,0:T(8,128)(2,1)}) %all-gather.23.cloned.1.call-update) | async-done | bytes 1966096 | tf_op jit(solution)/shard_map/all_gather | solution.py:173
  323.2 17.8 %all-gather.31.cloned.1.call-done = bf16[32,40,768]{2,1,0:T(8,128)(2,1)} async-done(((bf16[8,40,768]{2,1,0:T(8,128)(2,1)}), bf16[32,40,768]{2,1,0:T(8,128)(2,1)}) %all-gather.31.cloned.1.call-update) | async-done | bytes 1966096 | tf_op jit(solution)/shard_map/all_gather | solution.py:220
  341.0 7.0 fusion.13
  352.7 18.9 %all-gather.19.cloned.1.call-done = bf16[32,64,768]{2,1,0:T(8,128)(2,1)} async-done(((bf16[8,64,768]{2,1,0:T(8,128)(2,1)}), bf16[32,64,768]{2,1,0:T(8,128)(2,1)}) %all-gather.19.cloned.1.call-update) | async-done | bytes 3145744 | tf_op jit(solution)/shard_map/all_gather | solution.py:172
  371.7 7.5 fusion.85
  379.2 22.4 %all-gather.25.cloned.1.call-done = bf16[32,64,768]{2,1,0:T(8,128)(2,1)} async-done(((bf16[8,64,768]{2,1,0:T(8,128)(2,1)}), bf16[32,64,768]{2,1,0:T(8,128)(2,1)}) %all-gather.25.cloned.1.call-update) | async-done | bytes 3145744 | tf_op jit(solution)/shard_map/all_gather | solution.py:219
  401.7 8.5 fusion.6
  415.9 18.7 %reduce-scatter.29.cloned.1.call-done = bf16[8,40,768]{2,1,0:T(8,128)(2,1)} async-done(((bf16[32,40,768]{2,1,0:T(8,128)(2,1)}), bf16[8,40,768]{2,1,0:T(8,128)(2,1)}) %reduce-scatter.29.cloned.1.call-update) | async-done | bytes 491536 | tf_op jit(solution)/shard_map/reduce_scatter | solution.py:273
  439.9 35.0 %reduce-scatter.25.cloned.1.call-done = bf16[8,64,768]{2,1,0:T(8,128)(2,1)} async-done(((bf16[32,64,768]{2,1,0:T(8,128)(2,1)}), bf16[8,64,768]{2,1,0:T(8,128)(2,1)}) %reduce-scatter.25.cloned.1.call-update) | async-done | bytes 786448 | tf_op jit(solution)/shard_map/reduce_scatter | solution.py:270
  479.8 18.9 %all-gather.33.cloned.1.call-done = bf16[32,40,768]{2,1,0:T(8,128)(2,1)} async-done(((bf16[8,40,768]{2,1,0:T(8,128)(2,1)}), bf16[32,40,768]{2,1,0:T(8,128)(2,1)}) %all-gather.33.cloned.1.call-update) | async-done | bytes 1966096 | tf_op jit(solution)/shard_map/all_gather | solution.py:220
  578.4 8.7 convolution_convert_fusion.1
  590.3 10.0 reduce-scatter.23.cloned.1.call-done
  616.1 24.6 %reduce-scatter.27.cloned.1.call-done = bf16[8,64,768]{2,1,0:T(8,128)(2,1)} async-done(((bf16[32,64,768]{2,1,0:T(8,128)(2,1)}), bf16[8,64,768]{2,1,0:T(8,128)(2,1)}) %reduce-scatter.27.cloned.1.call-update) | async-done | bytes 786448 | tf_op jit(solution)/shard_map/reduce_scatter | solution.py:270
  643.9 37.2 %reduce-scatter.17.cloned.1.call-done = bf16[8,64,768]{2,1,0:T(8,128)(2,1)} async-done(((bf16[32,64,768]{2,1,0:T(8,128)(2,1)}), bf16[8,64,768]{2,1,0:T(8,128)(2,1)}) %reduce-scatter.17.cloned.1.call-update) | async-done | bytes 786448 | tf_op jit(solution)/shard_map/reduce_scatter | solution.py:197
  726.7 9.0 all-gather.29.cloned.1.call-done
  769.6 8.5 fusion.45
  849.5 10.7 all-reduce.2
  860.2 40.7 %all-reduce = (f32[6,768]{1,0:T(8,128)}, f32[6,768]{1,0:T(8,128)}) all-reduce(bf16[6,768]{1,0:T(8,128)(2,1)S(1)} %get-tuple-element.40, bf16[6,768]{1,0:T(8,128)(2,1)S(1)} %get-tuple-element.41), channel_id=1, replica_groups=mesh['dp'=8,'mp'=4] {'dp'}, use_global_device_ids=true, to_apply=%region_59.0 | all-reduce | flops 9216 | bytes 55296 | tf_op jit(solution)/shard_map/psum | solution.py:302
  903.9 241.7 %all-reduce.5.cloned.1.call-done = (bf16[4,768,3,192]{1,3,2,0:T(8,128)(2,1)}, bf16[4,192,768]{2,1,0:T(8,128)(2,1)}, bf16[2,768,768]{2,1,0:T(8,128)(2,1)}, bf16[2,768,768]{2,1,0:T(8,128)(2,1)}) async-done(((bf16[4,768,3,192]{1,3,2,0:T(8,128)(2,1)}, bf16[4,192,768]{2,1,0:T(8,128)(2,1)}, bf16[2,768,768]{2,1,0:T(8,128)(2,1)}, bf16[2,768,768]{2,1,0:T(8,128)(2,1)}), (bf16[4,768,3,192]{1,3,2,0:T(8,128)(2,1)}, ...) | async-done | bytes 9437200 | tf_op jit(solution)/shard_map/psum | solution.py:299
  (548 shorter events, 442.5 us)
Async XLA Ops:
  14.5 55.4 %all-gather.15.cloned.1.call-start = ((), (), s32[]{:S(2)}) async-start(), calls=%async_computation.13 | async-start | bytes 3932160 | tf_op jit(solution)/shard_map/all_gather | solution.py:172
  16.5 107.4 %reduce-scatter.19.cloned.1.call-start = ((), (), s32[]{:S(2)}) async-start(), calls=%async_computation.19 | async-start | bytes 2457600 | tf_op jit(solution)/shard_map/reduce_scatter | solution.py:200
  93.4 71.4 %reduce-scatter.13.cloned.1.call-start = ((), (), s32[]{:S(2)}) async-start(), calls=%async_computation.14 | async-start | bytes 3932160 | tf_op jit(solution)/shard_map/reduce_scatter | solution.py:197
  118.0 70.6 %all-gather.21.cloned.1.call-start = ((), (), s32[]{:S(2)}) async-start(), calls=%async_computation.20 | async-start | bytes 2457600 | tf_op jit(solution)/shard_map/all_gather | solution.py:173
  127.6 91.5 %all-gather.17.cloned.1.call-start = ((), (), s32[]{:S(2)}) async-start(), calls=%async_computation.15 | async-start | bytes 3932160 | tf_op jit(solution)/shard_map/all_gather | solution.py:172
  168.1 84.7 %reduce-scatter.21.cloned.1.call-start = ((), (), s32[]{:S(2)}) async-start(), calls=%async_computation.21 | async-start | bytes 2457600 | tf_op jit(solution)/shard_map/reduce_scatter | solution.py:200
  218.0 75.8 %reduce-scatter.15.cloned.1.call-start = ((), (), s32[]{:S(2)}) async-start(), calls=%async_computation.16 | async-start | bytes 3932160 | tf_op jit(solution)/shard_map/reduce_scatter | solution.py:197
  247.9 69.8 %all-gather.23.cloned.1.call-start = ((), (), s32[]{:S(2)}) async-start(), calls=%async_computation.22 | async-start | bytes 2457600 | tf_op jit(solution)/shard_map/all_gather | solution.py:173
  256.0 85.0 %all-gather.31.cloned.1.call-start = ((), (), s32[]{:S(2)}) async-start(), calls=%async_computation.29 | async-start | bytes 2457600 | tf_op jit(solution)/shard_map/all_gather | solution.py:220
  256.6 115.1 %all-gather.19.cloned.1.call-start = ((), (), s32[]{:S(2)}) async-start(), calls=%async_computation.17 | async-start | bytes 3932160 | tf_op jit(solution)/shard_map/all_gather | solution.py:172
  297.0 104.6 %all-gather.25.cloned.1.call-start = ((), (), s32[]{:S(2)}) async-start(), calls=%async_computation.24 | async-start | bytes 3932160 | tf_op jit(solution)/shard_map/all_gather | solution.py:219
  297.6 137.0 %reduce-scatter.29.cloned.1.call-start = ((), (), s32[]{:S(2)}) async-start(), calls=%async_computation.30 | async-start | bytes 2457600 | tf_op jit(solution)/shard_map/reduce_scatter | solution.py:273
  352.3 122.6 %reduce-scatter.25.cloned.1.call-start = ((), (), s32[]{:S(2)}) async-start(), calls=%async_computation.25 | async-start | bytes 3932160 | tf_op jit(solution)/shard_map/reduce_scatter | solution.py:270
  415.9 82.9 %all-gather.33.cloned.1.call-start = ((), (), s32[]{:S(2)}) async-start(), calls=%async_computation.31 | async-start | bytes 2457600 | tf_op jit(solution)/shard_map/all_gather | solution.py:220
  439.9 103.8 %all-gather.27.cloned.1.call-start = ((), (), s32[]{:S(2)}) async-start(), calls=%async_computation.26 | async-start | bytes 3932160 | tf_op jit(solution)/shard_map/all_gather | solution.py:219
  479.6 107.6 %reduce-scatter.31.cloned.1.call-start = ((), (), s32[]{:S(2)}) async-start(), calls=%async_computation.32 | async-start | bytes 2457600 | tf_op jit(solution)/shard_map/reduce_scatter | solution.py:273
  537.0 63.3 %reduce-scatter.23.cloned.1.call-start = ((), (), s32[]{:S(2)}) async-start(), calls=%async_computation.23 | async-start | bytes 2457600 | tf_op jit(solution)/shard_map/reduce_scatter | solution.py:200
  543.3 97.4 %reduce-scatter.27.cloned.1.call-start = ((), (), s32[]{:S(2)}) async-start(), calls=%async_computation.27 | async-start | bytes 3932160 | tf_op jit(solution)/shard_map/reduce_scatter | solution.py:270
  578.0 103.1 %reduce-scatter.17.cloned.1.call-start = ((), (), s32[]{:S(2)}) async-start(), calls=%async_computation.18 | async-start | bytes 3932160 | tf_op jit(solution)/shard_map/reduce_scatter | solution.py:197
  587.1 117.9 %all-gather.35.cloned.1.call-start = ((), (), s32[]{:S(2)}) async-start(), calls=%async_computation.33 | async-start | bytes 2457600 | tf_op jit(solution)/shard_map/all_gather | solution.py:220
  604.2 131.5 %all-gather.29.cloned.1.call-start = ((), (), s32[]{:S(2)}) async-start(), calls=%async_computation.28 | async-start | bytes 3932160 | tf_op jit(solution)/shard_map/all_gather | solution.py:219
  685.2 154.6 %reduce-scatter.35.cloned.1.call-start = ((), (), s32[]{:S(2)}) async-start(), calls=%async_computation.35 | async-start | bytes 2457600 | tf_op jit(solution)/shard_map/reduce_scatter | solution.py:273
  767.0 78.4 %reduce-scatter.33.cloned.1.call-start = ((), (), s32[]{:S(2)}) async-start(), calls=%async_computation.34 | async-start | bytes 3932160 | tf_op jit(solution)/shard_map/reduce_scatter | solution.py:270
  803.4 342.2 %all-reduce.5.cloned.1.call-start = ((), (), s32[]{:S(2)}) async-start(), calls=%async_computation.36 | async-start | bytes 18874368 | tf_op jit(solution)/shard_map/psum | solution.py:299
  (133 other events, 694.1 us)
Sparse Core Ops, SparseCore 0:
  14.7 24.5 all-gather.12
  41.4 28.4 all-gather.14
  93.5 30.3 reduce-scatter.18
  126.9 37.8 reduce-scatter.12
  190.6 28.4 all-gather.16
  222.3 30.3 reduce-scatter.20
  255.8 37.8 reduce-scatter.14
  295.9 21.8 all-gather.22
  319.2 21.8 all-gather.30
  343.2 28.4 all-gather.18
  373.1 28.4 all-gather.24
  404.2 30.3 reduce-scatter.28
  437.0 37.8 reduce-scatter.24
  476.9 21.8 all-gather.32
  500.8 28.4 all-gather.26
  537.1 30.3 reduce-scatter.30
  569.9 30.3 reduce-scatter.22
  602.8 37.8 reduce-scatter.26
  643.1 37.8 reduce-scatter.16
  683.2 21.8 all-gather.34
  707.2 28.4 all-gather.28
  767.1 30.3 reduce-scatter.34
  803.5 37.7 reduce-scatter.32
  846.3 299.1 all-reduce.4
  (1 shorter events, 21.8 us)
where the time goes:
time: 1170 us; the launch traced here: 1160 us
  waiting for transfers between devices  633 us (54%)
  matrix products  245 us (21%)
  local copies, waits for them, and re-layouts  130 us (11%)
  other arithmetic  84.9 us (7%)
  blocking collectives  51.5 us (4%)
  between operations  16 us (1%)
    psum x1, waiting for transfers between devices, per_device(): lax.psum(grad.astype(jnp.bfloat16), 'dp').astype(jnp.float32)  242 us
    reduce_scatter x6, waiting for transfers between devices, per_device(): lax.psum_scatter(text_part.astype(jnp.bfloat16), 'mp', scatter_dimension=...  171 us
    dot_general x20, matrix products, linear(): jnp.einsum('pld,de->ple', activation, weight, preferred_element_type=jnp....  82 us
    dot_general x20, matrix products, linear_back(): jnp.einsum('ple,de->pld', gradient, weight, preferred_element_type=jnp.fl...  68.1 us
    all_gather x3, waiting for transfers between devices, per_device(): lax.all_gather(visual_norm, 'mp', axis=0, tiled=True)  58.5 us
    all_gather x3, waiting for transfers between devices, per_device(): lax.all_gather(text_norm, 'mp', axis=0, tiled=True)  47.1 us
    all_gather x3, waiting for transfers between devices, per_device(): lax.all_gather(visual_back.astype(jnp.bfloat16), 'mp', axis=0, tiled=True)  42.2 us
    psum x1, blocking collectives, per_device(): gain_grads, shift_grads = lax.psum((gain_grads, shift_grads), 'dp')  40.7 us
  transfers between devices with their start and end apart: 25, of which 21 were waited for; matrix products, arithmetic and copies ran while one was open for 31% of the time, Pallas kernels for 0%

commit v1 on v0

--- a/solution.py
+++ b/solution.py
@@ -5,6 +5,27 @@
 
 HEAD = 64
 EPSILON = 1e-05
+
+
+def collect(value, axis, dim):
+    size, index, rows = (lax.axis_size(axis), lax.axis_index(axis), value.shape[dim])
+    forward = [(i, (i + 1) % size) for i in range(size)]
+    left = [(i, (i - 1) % size) for i in range(size)]
+    result = jnp.zeros((*value.shape[:dim], size * rows, *value.shape[dim + 1 :]), value.dtype)
+    result = lax.dynamic_update_slice_in_dim(result, value, index * rows, axis=dim)
+    from_left = from_right = value
+    middle = size // 2
+    for step in range(1, middle + 1):
+        from_left = lax.ppermute(from_left, axis, forward)
+        result = lax.dynamic_update_slice_in_dim(
+            result, from_left, (index - step) % size * rows, axis=dim
+        )
+        if step < size - middle:
+            from_right = lax.ppermute(from_right, axis, left)
+            result = lax.dynamic_update_slice_in_dim(
+                result, from_right, (index + step) % size * rows, axis=dim
+            )
+    return result
 
 
 def normalize(values, gain, shift):
@@ -217,7 +238,7 @@
     for sublayer in (2, 1, 0):
         text_branch, visual_branch = (
             lax.all_gather(text_back.astype(jnp.bfloat16), "mp", axis=0, tiled=True),
-            lax.all_gather(visual_back.astype(jnp.bfloat16), "mp", axis=0, tiled=True),
+            collect(visual_back.astype(jnp.bfloat16), "mp", 0),
         )
         text_rows, visual_rows = gathered[sublayer]
         text_saved, visual_saved = saved[sublayer]

time: 1170 us -> 1120 us (0.957)
  waiting for transfers between devices: 633 us -> 580 us
    ppermute x0 -> x9, waiting for transfers between devices: none -> 75.8 us  [the longest x6 69.9 us: collect(): from_left = lax.ppermute(from_left, axis, forward)]
    reduce_scatter x6, waiting for transfers between devices: 171 us -> 113 us  [per_device(): lax.psum_scatter(text_part.astype(jnp.bfloat16), 'mp', scatter_dimension=...]
    all_gather x3 -> x0, waiting for transfers between devices: 42.2 us -> none  [per_device(): lax.all_gather(visual_back.astype(jnp.bfloat16), 'mp', axis=0, tiled=True)]
    all_gather x3, waiting for transfers between devices: 47.1 us -> 24.3 us  [per_device(): lax.all_gather(text_norm, 'mp', axis=0, tiled=True)]
    reduce_scatter x6, waiting for transfers between devices: 39.3 us -> 61.9 us  [per_device(): lax.psum_scatter(visual_part.astype(jnp.bfloat16), 'mp', scatter_dimensio...]
    all_gather x3, waiting for transfers between devices: 58.5 us -> 38.4 us  [per_device(): lax.all_gather(visual_norm, 'mp', axis=0, tiled=True)]
    unnamed x264 -> x282, local copies, waits for them, and re-layouts: 27.2 us -> 29.8 us
  transfers between devices with their start and end apart: 25 -> 31, of which waited for: 21 -> 21; matrix products, arithmetic and copies ran while one was open for 31% -> 33% of each run, Pallas kernels for 0% -> 0%
where the time goes in v1:
time: 1120 us; the launch traced here: 1110 us
  waiting for transfers between devices  580 us (52%)
  matrix products  243 us (22%)
  local copies, waits for them, and re-layouts  132 us (12%)
  other arithmetic  81.3 us (7%)
  blocking collectives  51.8 us (5%)
  between operations  16.5 us (1%)
    psum x1, waiting for transfers between devices, per_device(): lax.psum(grad.astype(jnp.bfloat16), 'dp').astype(jnp.float32)  242 us
    reduce_scatter x6, waiting for transfers between devices, per_device(): lax.psum_scatter(text_part.astype(jnp.bfloat16), 'mp', scatter_dimension=...  113 us
    dot_general x20, matrix products, linear(): jnp.einsum('pld,de->ple', activation, weight, preferred_element_type=jnp....  78.7 us
    ppermute x6, waiting for transfers between devices, collect(): from_left = lax.ppermute(from_left, axis, forward)  69.9 us
    dot_general x20, matrix products, linear_back(): jnp.einsum('ple,de->pld', gradient, weight, preferred_element_type=jnp.fl...  66.4 us
    reduce_scatter x6, waiting for transfers between devices, per_device(): lax.psum_scatter(visual_part.astype(jnp.bfloat16), 'mp', scatter_dimensio...  61.9 us
    psum x1, blocking collectives, per_device(): gain_grads, shift_grads = lax.psum((gain_grads, shift_grads), 'dp')  41.2 us
    dot_general x20, matrix products, weight_grad(): jnp.einsum('pld,ple->de', activation, gradient, preferred_element_type=jn...  40.3 us
  transfers between devices with their start and end apart: 31, of which 21 were waited for; matrix products, arithmetic and copies ran while one was open for 33% of the time, Pallas kernels for 0%

profile of v1, /device:TPU:0, one launch (start us, length us, event | category | flops | bytes accessed | tf_op | source)
XLA Modules:
  0.0 1113.5 jit_solution(6706882108421482345)
XLA Ops:
  20.6 18.7 %all-gather.10.cloned.1.call-done = bf16[32,40,768]{2,1,0:T(8,128)(2,1)} async-done(((bf16[8,40,768]{2,1,0:T(8,128)(2,1)}), bf16[32,40,768]{2,1,0:T(8,128)(2,1)}) %all-gather.10.cloned.1.call-update) | async-done | bytes 1966096 | tf_op jit(solution)/shard_map/all_gather | solution.py:194
  46.3 23.6 %all-gather.12.cloned.1.call-done = bf16[32,64,768]{2,1,0:T(8,128)(2,1)} async-done(((bf16[8,64,768]{2,1,0:T(8,128)(2,1)}), bf16[32,64,768]{2,1,0:T(8,128)(2,1)}) %all-gather.12.cloned.1.call-update) | async-done | bytes 3145744 | tf_op jit(solution)/shard_map/all_gather | solution.py:193
  86.9 38.0 %reduce-scatter.13.cloned.1.call-done = bf16[8,64,768]{2,1,0:T(8,128)(2,1)} async-done(((bf16[32,64,768]{2,1,0:T(8,128)(2,1)}), bf16[8,64,768]{2,1,0:T(8,128)(2,1)}) %reduce-scatter.13.cloned.1.call-update) | async-done | bytes 786448 | tf_op jit(solution)/shard_map/reduce_scatter | solution.py:218
  182.2 8.1 reduce-scatter.19.cloned.1.call-done
  194.0 37.1 %reduce-scatter.15.cloned.1.call-done = bf16[8,64,768]{2,1,0:T(8,128)(2,1)} async-done(((bf16[32,64,768]{2,1,0:T(8,128)(2,1)}), bf16[8,64,768]{2,1,0:T(8,128)(2,1)}) %reduce-scatter.15.cloned.1.call-update) | async-done | bytes 786448 | tf_op jit(solution)/shard_map/reduce_scatter | solution.py:218
  235.4 19.8 %all-gather.18.cloned.1.call-done = bf16[32,40,768]{2,1,0:T(8,128)(2,1)} async-done(((bf16[8,40,768]{2,1,0:T(8,128)(2,1)}), bf16[32,40,768]{2,1,0:T(8,128)(2,1)}) %all-gather.18.cloned.1.call-update) | async-done | bytes 1966096 | tf_op jit(solution)/shard_map/all_gather | solution.py:194
  289.0 7.6 fusion.85
  296.6 19.3 %all-gather.22.cloned.1.call-done = bf16[32,64,768]{2,1,0:T(8,128)(2,1)} async-done(((bf16[8,64,768]{2,1,0:T(8,128)(2,1)}), bf16[32,64,768]{2,1,0:T(8,128)(2,1)}) %all-gather.22.cloned.1.call-update) | async-done | bytes 3145744 | tf_op jit(solution)/shard_map/all_gather | solution.py:240
  315.9 8.5 fusion.6
  330.1 18.6 %reduce-scatter.21.cloned.1.call-done = bf16[8,40,768]{2,1,0:T(8,128)(2,1)} async-done(((bf16[32,40,768]{2,1,0:T(8,128)(2,1)}), bf16[8,40,768]{2,1,0:T(8,128)(2,1)}) %reduce-scatter.21.cloned.1.call-update) | async-done | bytes 491536 | tf_op jit(solution)/shard_map/reduce_scatter | solution.py:221
  352.1 37.7 %reduce-scatter.25.cloned.1.call-done = bf16[8,64,768]{2,1,0:T(8,128)(2,1)} async-done(((bf16[32,64,768]{2,1,0:T(8,128)(2,1)}), bf16[8,64,768]{2,1,0:T(8,128)(2,1)}) %reduce-scatter.25.cloned.1.call-update) | async-done | bytes 786448 | tf_op jit(solution)/shard_map/reduce_scatter | solution.py:291
  396.3 17.5 %collective-permute-done = bf16[8,40,768]{2,1,0:T(8,128)(2,1)} collective-permute-done((bf16[8,40,768]{2,1,0:T(8,128)(2,1)}, bf16[8,40,768]{2,1,0:T(8,128)(2,1)}, u32[]{:S(2)}, u32[]{:S(2)}) %collective-permute-start) | collective-permute-done | bytes 491552 | tf_op jit(solution)/shard_map/ppermute | solution.py:19
  429.8 7.8 fusion.13
  487.7 8.6 convolution_convert_fusion.1
  498.2 20.1 %reduce-scatter.23.cloned.1.call-done = bf16[8,40,768]{2,1,0:T(8,128)(2,1)} async-done(((bf16[32,40,768]{2,1,0:T(8,128)(2,1)}), bf16[8,40,768]{2,1,0:T(8,128)(2,1)}) %reduce-scatter.23.cloned.1.call-update) | async-done | bytes 491536 | tf_op jit(solution)/shard_map/reduce_scatter | solution.py:221
  523.7 11.1 collective-permute-done.3
  534.9 13.3 %collective-permute-done.5 = bf16[8,40,768]{2,1,0:T(8,128)(2,1)S(1)} collective-permute-done((bf16[8,40,768]{2,1,0:T(8,128)(2,1)S(1)}, bf16[8,40,768]{2,1,0:T(8,128)(2,1)S(1)}, u32[]{:S(2)}, u32[]{:S(2)}) %collective-permute-start.5) | collective-permute-done | bytes 491552 | tf_op jit(solution)/shard_map/ppermute | solution.py:19
  619.2 15.0 %reduce-scatter.31.cloned.1.call-done = bf16[8,40,768]{2,1,0:T(8,128)(2,1)} async-done(((bf16[32,40,768]{2,1,0:T(8,128)(2,1)}), bf16[8,40,768]{2,1,0:T(8,128)(2,1)}) %reduce-scatter.31.cloned.1.call-update) | async-done | bytes 491536 | tf_op jit(solution)/shard_map/reduce_scatter | solution.py:294
  643.9 11.7 %collective-permute-done.6 = bf16[8,40,768]{2,1,0:T(8,128)(2,1)S(1)} collective-permute-done((bf16[8,40,768]{2,1,0:T(8,128)(2,1)S(1)}, bf16[8,40,768]{2,1,0:T(8,128)(2,1)S(1)}, u32[]{:S(2)}, u32[]{:S(2)}) %collective-permute-start.6) | collective-permute-done | bytes 491552 | tf_op jit(solution)/shard_map/ppermute | solution.py:19
  663.1 12.1 %collective-permute-done.8 = bf16[8,40,768]{2,1,0:T(8,128)(2,1)S(1)} collective-permute-done((bf16[8,40,768]{2,1,0:T(8,128)(2,1)S(1)}, bf16[8,40,768]{2,1,0:T(8,128)(2,1)S(1)}, u32[]{:S(2)}, u32[]{:S(2)}) %collective-permute-start.8) | collective-permute-done | bytes 491552 | tf_op jit(solution)/shard_map/ppermute | solution.py:19
  718.8 8.5 fusion.45
  797.6 10.7 all-reduce.2
  808.3 41.2 %all-reduce = (f32[6,768]{1,0:T(8,128)}, f32[6,768]{1,0:T(8,128)}) all-reduce(bf16[6,768]{1,0:T(8,128)(2,1)S(1)} %get-tuple-element.40, bf16[6,768]{1,0:T(8,128)(2,1)S(1)} %get-tuple-element.41), channel_id=1, replica_groups=mesh['dp'=8,'mp'=4] {'dp'}, use_global_device_ids=true, to_apply=%region_59.60 | all-reduce | flops 9216 | bytes 55296 | tf_op jit(solution)/shard_map/psum | solution.py:323
  852.4 242.3 %all-reduce.5.cloned.1.call-done = (bf16[4,768,3,192]{1,3,2,0:T(8,128)(2,1)}, bf16[4,192,768]{2,1,0:T(8,128)(2,1)}, bf16[2,768,768]{2,1,0:T(8,128)(2,1)}, bf16[2,768,768]{2,1,0:T(8,128)(2,1)}) async-done(((bf16[4,768,3,192]{1,3,2,0:T(8,128)(2,1)}, bf16[4,192,768]{2,1,0:T(8,128)(2,1)}, bf16[2,768,768]{2,1,0:T(8,128)(2,1)}, bf16[2,768,768]{2,1,0:T(8,128)(2,1)}), (bf16[4,768,3,192]{1,3,2,0:T(8,128)(2,1)}, ...) | async-done | bytes 9437200 | tf_op jit(solution)/shard_map/psum | solution.py:320
  (586 shorter events, 440.1 us)
Async XLA Ops:
  7.2 32.1 %all-gather.10.cloned.1.call-start = ((), (), s32[]{:S(2)}) async-start(), calls=%async_computation.12 | async-start | bytes 2457600 | tf_op jit(solution)/shard_map/all_gather | solution.py:194
  14.5 55.4 %all-gather.12.cloned.1.call-start = ((), (), s32[]{:S(2)}) async-start(), calls=%async_computation.13 | async-start | bytes 3932160 | tf_op jit(solution)/shard_map/all_gather | solution.py:193
  16.5 108.4 %reduce-scatter.13.cloned.1.call-start = ((), (), s32[]{:S(2)}) async-start(), calls=%async_computation.14 | async-start | bytes 3932160 | tf_op jit(solution)/shard_map/reduce_scatter | solution.py:218
  86.9 70.0 %all-gather.14.cloned.1.call-start = ((), (), s32[]{:S(2)}) async-start(), calls=%async_computation.15 | async-start | bytes 3932160 | tf_op jit(solution)/shard_map/all_gather | solution.py:193
  128.2 62.1 %reduce-scatter.19.cloned.1.call-start = ((), (), s32[]{:S(2)}) async-start(), calls=%async_computation.19 | async-start | bytes 2457600 | tf_op jit(solution)/shard_map/reduce_scatter | solution.py:221
  155.6 75.5 %reduce-scatter.15.cloned.1.call-start = ((), (), s32[]{:S(2)}) async-start(), calls=%async_computation.16 | async-start | bytes 3932160 | tf_op jit(solution)/shard_map/reduce_scatter | solution.py:218
  182.1 73.0 %all-gather.18.cloned.1.call-start = ((), (), s32[]{:S(2)}) async-start(), calls=%async_computation.20 | async-start | bytes 2457600 | tf_op jit(solution)/shard_map/all_gather | solution.py:194
  194.0 95.0 %all-gather.16.cloned.1.call-start = ((), (), s32[]{:S(2)}) async-start(), calls=%async_computation.17 | async-start | bytes 3932160 | tf_op jit(solution)/shard_map/all_gather | solution.py:193
  234.4 81.5 %all-gather.22.cloned.1.call-start = ((), (), s32[]{:S(2)}) async-start(), calls=%async_computation.24 | async-start | bytes 3932160 | tf_op jit(solution)/shard_map/all_gather | solution.py:240
  235.2 113.6 %reduce-scatter.21.cloned.1.call-start = ((), (), s32[]{:S(2)}) async-start(), calls=%async_computation.21 | async-start | bytes 2457600 | tf_op jit(solution)/shard_map/reduce_scatter | solution.py:221
  288.7 101.1 %reduce-scatter.25.cloned.1.call-start = ((), (), s32[]{:S(2)}) async-start(), calls=%async_computation.25 | async-start | bytes 3932160 | tf_op jit(solution)/shard_map/reduce_scatter | solution.py:291
  330.1 95.9 %all-gather.20.cloned.1.call-start = ((), (), s32[]{:S(2)}) async-start(), calls=%async_computation.22 | async-start | bytes 2457600 | tf_op jit(solution)/shard_map/all_gather | solution.py:194
  352.0 100.6 %all-gather.24.cloned.1.call-start = ((), (), s32[]{:S(2)}) async-start(), calls=%async_computation.26 | async-start | bytes 3932160 | tf_op jit(solution)/shard_map/all_gather | solution.py:240
  394.5 102.0 %reduce-scatter.29.cloned.1.call-start = ((), (), s32[]{:S(2)}) async-start(), calls=%async_computation.29 | async-start | bytes 2457600 | tf_op jit(solution)/shard_map/reduce_scatter | solution.py:294
  394.6 23.6 %collective-permute-start.1 = (bf16[8,40,768]{2,1,0:T(8,128)(2,1)}, bf16[8,40,768]{2,1,0:T(8,128)(2,1)}, u32[]{:S(2)}, u32[]{:S(2)}) collective-permute-start(bf16[8,40,768]{2,1,0:T(8,128)(2,1)} %param.21), channel_id=1, source_target_pairs={{0,3},{1,0},{2,1},{3,2},{4,7},{5,4},{6,5},{7,6},{8,11},{9,8},{10,9... | collective-permute-start | bytes 1474568 | tf_op jit(solution)/shard_map/ppermute | solution.py:24
  442.0 76.4 %reduce-scatter.23.cloned.1.call-start = ((), (), s32[]{:S(2)}) async-start(), calls=%async_computation.23 | async-start | bytes 2457600 | tf_op jit(solution)/shard_map/reduce_scatter | solution.py:221
  448.4 156.1 %reduce-scatter.27.cloned.1.call-start = ((), (), s32[]{:S(2)}) async-start(), calls=%async_computation.27 | async-start | bytes 3932160 | tf_op jit(solution)/shard_map/reduce_scatter | solution.py:291
  487.5 120.7 %reduce-scatter.17.cloned.1.call-start = ((), (), s32[]{:S(2)}) async-start(), calls=%async_computation.18 | async-start | bytes 3932160 | tf_op jit(solution)/shard_map/reduce_scatter | solution.py:218
  496.4 137.8 %reduce-scatter.31.cloned.1.call-start = ((), (), s32[]{:S(2)}) async-start(), calls=%async_computation.30 | async-start | bytes 2457600 | tf_op jit(solution)/shard_map/reduce_scatter | solution.py:294
  586.8 106.5 %all-gather.26.cloned.1.call-start = ((), (), s32[]{:S(2)}) async-start(), calls=%async_computation.28 | async-start | bytes 3932160 | tf_op jit(solution)/shard_map/all_gather | solution.py:240
  612.7 175.2 %reduce-scatter.35.cloned.1.call-start = ((), (), s32[]{:S(2)}) async-start(), calls=%async_computation.32 | async-start | bytes 2457600 | tf_op jit(solution)/shard_map/reduce_scatter | solution.py:294
  641.0 22.0 %collective-permute-start.7 = (bf16[8,40,768]{2,1,0:T(8,128)(2,1)S(1)}, bf16[8,40,768]{2,1,0:T(8,128)(2,1)S(1)}, u32[]{:S(2)}, u32[]{:S(2)}) collective-permute-start(bf16[8,40,768]{2,1,0:T(8,128)(2,1)S(1)} %get-tuple-element.43), channel_id=1, source_target_pairs={{0,3},{1,0},{2,1},{3,2},{4,7},{5,4},{6,5},{7,6},{8,11},{9,8},{10,9... | collective-permute-start | bytes 1474568 | tf_op jit(solution)/shard_map/ppermute | solution.py:24
  716.7 76.8 %reduce-scatter.33.cloned.1.call-start = ((), (), s32[]{:S(2)}) async-start(), calls=%async_computation.31 | async-start | bytes 3932160 | tf_op jit(solution)/shard_map/reduce_scatter | solution.py:291
  752.7 342.0 %all-reduce.5.cloned.1.call-start = ((), (), s32[]{:S(2)}) async-start(), calls=%async_computation.33 | async-start | bytes 18874368 | tf_op jit(solution)/shard_map/psum | solution.py:320
  (148 other events, 807.9 us)
Sparse Core Ops, SparseCore 0:
  14.7 24.5 all-gather.9
  41.4 28.4 all-gather.11
  87.0 37.8 reduce-scatter.12
  128.3 28.5 all-gather.13
  159.8 30.3 reduce-scatter.18
  193.2 37.8 reduce-scatter.14
  233.3 21.8 all-gather.17
  257.3 28.4 all-gather.15
  287.4 28.4 all-gather.21
  318.3 30.3 reduce-scatter.20
  351.9 37.8 reduce-scatter.24
  391.8 29.3 all-gather.19
  423.3 29.3 all-gather.23
  455.1 30.3 reduce-scatter.28
  487.9 30.3 reduce-scatter.22
  520.7 40.5 reduce-scatter.26
  563.7 37.6 reduce-scatter.16
  603.8 30.3 reduce-scatter.30
  636.4 40.1 all-gather.25
  716.8 30.3 reduce-scatter.34
  752.8 37.5 reduce-scatter.32
  795.4 299.2 all-reduce.4
